TPU v7x, 32 devices: a whole 2x2x4 slice. The times are simulated.
32 devices in a mesh: fsdp: 8 (over z, y), dp: 4 (over x, core).
Axes of the slice: x: 2, y: 2, z: 4, core: 2. Of those that a mesh axis runs over, the one named last changes fastest.
Arguments:
- hidden_in: bfloat16 [128, 128, 768], P(('fsdp', 'dp')), may hold values from -6 to 6
- query_key_value_weight: bfloat16 [768, 2304], P('fsdp'), may hold values from -0.21875 to 0.21875
- attention_output_weight: bfloat16 [768, 768], P('fsdp'), may hold values from -0.625 to 0.625
- gate_up_weight: bfloat16 [768, 6144], P('fsdp'), may hold values from -0.21875 to 0.21875
- down_weight: bfloat16 [3072, 768], P('fsdp'), may hold values from -0.109375 to 0.109375
- gain_attn: bfloat16 [768], P('fsdp'), may hold values from 0.25 to 1.75
- shift_attn: bfloat16 [768], P('fsdp'), may hold values from -3 to 3
- gain_ffn: bfloat16 [768], P('fsdp'), may hold values from 0.25 to 1.75
- shift_ffn: bfloat16 [768], P('fsdp'), may hold values from -3 to 3
- masked_output_gradient: bfloat16 [128, 32, 768], P(('fsdp', 'dp')), may hold values from -6 to 6
- positions: int32 [128, 32], P(('fsdp', 'dp')), may hold values from 0 to 127, as said below
- mask_counts: int32 [128], P(('fsdp', 'dp')), may hold values from 8 to 32
Outputs:
- layer_out: bfloat16 [128, 128, 768], P(('fsdp', 'dp'))
- grad_in: float32 [128, 128, 768], P(('fsdp', 'dp'))
- grad_qkv: float32 [768, 2304], P('fsdp')
- grad_out_proj: float32 [768, 768], P('fsdp')
- grad_up: float32 [768, 6144], P('fsdp')
- grad_down: float32 [3072, 768], P('fsdp')
- grad_gain_attn: float32 [768], P('fsdp')
- grad_shift_attn: float32 [768], P('fsdp')
- grad_gain_ffn: float32 [768], P('fsdp')
- grad_shift_ffn: float32 [768], P('fsdp')
Inputs may be any that keep to these rules, and one draw needn't show every extreme that they name: Within one sequence the listed positions are distinct.
All inputs are finite; a program needn't handle non-finite values.
Results may differ from a plain program's by a relative error of at most 0.015.
Values may be sent and summed in bfloat16 or wider, within the bound.
No kernel may reach another device: no remote copies, remote signals or barrier semaphores. Data moves between devices by JAX's collectives and lax.ppermute only.
A program may use at most 192 MiB of HBM per device.

v0:
```python
import jax
import jax.numpy as jnp
from jax import lax
from jax.sharding import PartitionSpec as P

HEADS = 12
HEAD_DIM = 64
FF = 3072
EPS = 1e-12
F32 = jnp.float32
LOW = jnp.bfloat16
AXES = ("fsdp", "dp")


def mm(a, b):
    return jnp.dot(a, b, preferred_element_type=F32)


def slopes():
    return jnp.exp2(-8.0 * (jnp.arange(HEADS, dtype=F32) + 1.0) / HEADS)


def norm_parts(value):
    center = value - jnp.mean(value, axis=-1, keepdims=True)
    rstd = lax.rsqrt(jnp.mean(center * center, axis=-1, keepdims=True) + EPS)
    return (center * rstd, rstd)


def norm_back(grad, unit, rstd, gain):
    scaled = grad * gain
    return rstd * (
        scaled
        - jnp.mean(scaled, axis=-1, keepdims=True)
        - unit * jnp.mean(scaled * unit, axis=-1, keepdims=True)
    )


def pick(onehot, rows):
    if rows.dtype == LOW:
        return jnp.einsum(
            "svj,sjd->svd", onehot.astype(LOW), rows, preferred_element_type=F32
        ).astype(LOW)
    return jnp.einsum("svj,sjd->svd", onehot, rows, precision=lax.Precision.HIGHEST)


def gather_weights(w_qkv, w_out, w_up, w_down):
    fsdp = lax.axis_size("fsdp")
    dp = lax.axis_size("dp")
    rows, width = w_out.shape
    if rows % (8 * dp):
        return (
            lax.all_gather(w_qkv, "fsdp", axis=0, tiled=True),
            lax.all_gather(w_out, "fsdp", axis=0, tiled=True),
            lax.all_gather(w_up, "fsdp", axis=0, tiled=True),
            lax.all_gather(w_down, "fsdp", axis=0, tiled=True),
        )
    mine = lax.axis_index("dp")
    part = rows // dp
    group = w_down.shape[0] // rows
    joined = jnp.concatenate([w_qkv, w_out, w_up], axis=1)
    joined = lax.dynamic_slice_in_dim(joined, mine * part, part, axis=0)
    down = lax.dynamic_slice_in_dim(w_down, mine * part * group, part * group, axis=0)
    down = jnp.concatenate([down[k * part : (k + 1) * part] for k in range(group)], axis=1)
    full = lax.all_gather(jnp.concatenate([joined, down], axis=1), AXES, axis=0, tiled=True)
    a, b = (w_qkv.shape[1], w_qkv.shape[1] + w_out.shape[1])
    c = b + w_up.shape[1]
    full_down = full[:, c:].reshape(fsdp * dp, part, group, width)
    full_down = full_down.transpose(0, 2, 1, 3).reshape(fsdp * dp * part * group, width)
    return (full[:, :a], full[:, a:b], full[:, b:c], full_down)


def scatter_grads(g_qkv, g_out, g_up, g_down):
    fsdp = lax.axis_size("fsdp")
    dp = lax.axis_size("dp")
    width = g_out.shape[1]
    rows = g_out.shape[0] // fsdp
    if rows % (8 * dp):
        return tuple(
            (
                lax.psum(lax.psum_scatter(g, "fsdp", scatter_dimension=0, tiled=True), "dp")
                for g in (g_qkv, g_out, g_up, g_down)
            )
        )
    part = rows // dp
    group = g_down.shape[0] // g_out.shape[0]
    down = g_down.reshape(fsdp * dp, group, part, width).transpose(0, 2, 1, 3)
    down = down.reshape(fsdp * rows, group * width)
    joined = jnp.concatenate([g_qkv, g_out, g_up, down], axis=1).astype(LOW)
    mine = lax.psum_scatter(joined, AXES, scatter_dimension=0, tiled=True)
    full = lax.all_gather(mine, "dp", axis=0, tiled=True).astype(F32)
    a, b = (g_qkv.shape[1], g_qkv.shape[1] + width)
    c = b + g_up.shape[1]
    full_down = full[:, c:].reshape(dp, part, group, width).transpose(0, 2, 1, 3)
    return (full[:, :a], full[:, a:b], full[:, b:c], full_down.reshape(rows * group, width))


def on_device(
    hidden_in,
    w_qkv,
    w_out,
    w_up,
    w_down,
    gain_attn,
    shift_attn,
    gain_ffn,
    shift_ffn,
    grad_listed,
    positions,
    counts,
):
    seqs, length, width = hidden_in.shape
    tokens = seqs * length
    most = positions.shape[1]
    norms = jnp.stack([gain_attn, shift_attn, gain_ffn, shift_ffn])
    norms = lax.all_gather(norms, "fsdp", axis=1, tiled=True).astype(F32)
    w_qkv, w_out, w_up, w_down = gather_weights(w_qkv, w_out, w_up, w_down)
    live = jnp.arange(most, dtype=jnp.int32)[None, :] < counts[:, None]
    onehot = (positions[:, :, None] == jnp.arange(length, dtype=jnp.int32)).astype(F32)
    rows_in = hidden_in.reshape(tokens, width)
    slope = slopes()
    scale = HEAD_DIM ** (-0.5)
    qkv = mm(rows_in, w_qkv).astype(LOW)
    split = qkv.reshape(seqs, length, 3, HEADS, HEAD_DIM)
    q, k, v = (split[:, :, 0], split[:, :, 1], split[:, :, 2])
    place = jnp.arange(length, dtype=F32)
    bias = -slope[:, None, None] * jnp.abs(place[:, None] - place[None, :])
    s = jnp.einsum("sqhc,skhc->shqk", q, k, preferred_element_type=F32) * scale + bias
    p = jax.nn.softmax(s, axis=-1).astype(LOW)
    att = jnp.einsum("shqk,skhc->sqhc", p, v, preferred_element_type=F32).astype(LOW)
    att = att.reshape(tokens, width)
    r1 = rows_in.astype(F32) + mm(att, w_out)
    unit1, _ = norm_parts(r1)
    h1 = unit1 * norms[0] + norms[1]
    h1_low = h1.astype(LOW)
    u = mm(h1_low, w_up)
    act = (jax.nn.gelu(u[:, :FF], approximate=False) * u[:, FF:]).astype(LOW)
    r2 = h1 + mm(act, w_down)
    unit2, _ = norm_parts(r2)
    layer_out = (unit2 * norms[2] + norms[3]).astype(LOW).reshape(seqs, length, width)

    def listed(a):
        return pick(onehot, a.reshape(seqs, length, -1)).reshape(seqs * most, -1)

    dy = jnp.where(live[:, :, None], grad_listed, 0).astype(F32).reshape(seqs * most, width)
    unit2_m, rstd2_m = norm_parts(listed(r2))
    g_gain_ffn = jnp.sum(dy * unit2_m, axis=0)
    g_shift_ffn = jnp.sum(dy, axis=0)
    dr2 = norm_back(dy, unit2_m, rstd2_m, norms[2])
    e2 = dr2.astype(LOW)
    h1_m = listed(h1_low)
    u_m = mm(h1_m, w_up)
    gate, up = (u_m[:, :FF], u_m[:, FF:])
    cdf = 0.5 * (1.0 + lax.erf(gate * 0.5**0.5))
    pdf = jnp.exp(-0.5 * gate * gate) * (2.0 * jnp.pi) ** (-0.5)
    gelu = gate * cdf
    act_m = (gelu * up).astype(LOW)
    g_down = jnp.einsum("nf,nd->fd", act_m, e2, preferred_element_type=F32)
    dact = jnp.einsum("nd,fd->nf", e2, w_down, preferred_element_type=F32)
    du = jnp.concatenate([dact * up * (cdf + gate * pdf), dact * gelu], axis=1).astype(LOW)
    g_up = jnp.einsum("nd,nf->df", h1_m, du, preferred_element_type=F32)
    dh1 = dr2 + jnp.einsum("nf,df->nd", du, w_up, preferred_element_type=F32)
    unit1_m, rstd1_m = norm_parts(listed(r1))
    g_gain_attn = jnp.sum(dh1 * unit1_m, axis=0)
    g_shift_attn = jnp.sum(dh1, axis=0)
    dr1 = norm_back(dh1, unit1_m, rstd1_m, norms[0])
    e1 = dr1.astype(LOW)
    g_out = jnp.einsum("nd,ne->de", listed(att), e1, preferred_element_type=F32)
    datt = jnp.einsum("ne,de->nd", e1, w_out, preferred_element_type=F32).astype(LOW)
    datt = datt.reshape(seqs, most, HEADS, HEAD_DIM)
    q_m = listed(qkv[:, :width]).reshape(seqs, most, HEADS, HEAD_DIM)
    away = jnp.abs(positions[:, :, None].astype(F32) - place[None, None, :])
    s_m = jnp.einsum("sqhc,skhc->shqk", q_m, k, preferred_element_type=F32) * scale
    p_m = jax.nn.softmax(s_m - slope[None, :, None, None] * away[:, None], axis=-1)
    dv = jnp.einsum("shqk,sqhc->skhc", p_m.astype(LOW), datt, preferred_element_type=F32)
    dp = jnp.einsum("sqhc,skhc->shqk", datt, v, preferred_element_type=F32)
    ds = (p_m * (dp - jnp.sum(dp * p_m, axis=-1, keepdims=True))).astype(LOW)
    dq_m = (jnp.einsum("shqk,skhc->sqhc", ds, k, preferred_element_type=F32) * scale).astype(LOW)
    dk = (jnp.einsum("shqk,sqhc->skhc", ds, q_m, preferred_element_type=F32) * scale).astype(LOW)
    put = (onehot * live[:, :, None]).astype(LOW)
    dq = jnp.einsum(
        "svj,svd->sjd", put, dq_m.reshape(seqs, most, width), preferred_element_type=F32
    )
    dqkv = jnp.concatenate(
        [
            dq.astype(LOW).reshape(tokens, width),
            dk.reshape(tokens, width),
            dv.astype(LOW).reshape(tokens, width),
        ],
        axis=1,
    )
    g_qkv = jnp.einsum("nd,ne->de", rows_in, dqkv, preferred_element_type=F32)
    dr1_all = jnp.einsum(
        "svj,svd->sjd",
        onehot * live[:, :, None],
        dr1.reshape(seqs, most, width),
        precision=lax.Precision.HIGHEST,
    )
    grad_in = dr1_all.reshape(tokens, width) + jnp.einsum(
        "ne,de->nd", dqkv, w_qkv, preferred_element_type=F32
    )
    owned = scatter_grads(g_qkv, g_out, g_up, g_down)
    small = lax.psum(jnp.stack([g_gain_attn, g_shift_attn, g_gain_ffn, g_shift_ffn]), AXES)
    share = width // lax.axis_size("fsdp")
    small = lax.dynamic_slice_in_dim(small, lax.axis_index("fsdp") * share, share, axis=1)
    return (
        layer_out,
        grad_in.reshape(seqs, length, width),
        *owned,
        small[0],
        small[1],
        small[2],
        small[3],
    )


def solution(mesh):
    rows3 = P(("fsdp", "dp"), None, None)
    rows2 = P("fsdp", None)
    rows1 = P("fsdp")
    return jax.shard_map(
        on_device,
        mesh=mesh,
        in_specs=(
            rows3,
            rows2,
            rows2,
            rows2,
            rows2,
            rows1,
            rows1,
            rows1,
            rows1,
            rows3,
            P(("fsdp", "dp"), None),
            P(("fsdp", "dp")),
        ),
        out_specs=(rows3, rows3, rows2, rows2, rows2, rows2, rows1, rows1, rows1, rows1),
        check_vma=False,
    )
```

profile of v0, /device:TPU:0, one launch (start us, length us, event | category | flops | bytes accessed | tf_op | source)
XLA Modules:
  0.0 575.9 jit_solution(14297018178041532854)
XLA Ops:
  13.0 22.6 %all-gather = bf16[8,96,4]{1,2,0:T(4,128)(2,1)S(1)} all-gather(bf16[1,96,4]{1,2,0:T(4,128)(2,1)S(1)} %maximum_bitcast_fusion), channel_id=1, replica_groups=mesh['fsdp'=8,'dp'=4] {'fsdp'}, dimensions={0}, use_global_device_ids=true | all-gather | bytes 6912 | tf_op jit(solution)/shard_map/all_gather | solution.py:115
  40.1 99.0 %all-gather.4.cloned.1.call-done = bf16[768,12288]{1,0:T(8,128)(2,1)} async-done(((bf16[24,12288]{1,0:T(8,128)(2,1)}), bf16[768,12288]{1,0:T(8,128)(2,1)}) %all-gather.4.cloned.1.call-update) | async-done | bytes 18874384 | tf_op jit(solution)/shard_map/all_gather | solution.py:64
  139.1 4.8 slice.124
  144.0 9.7 %reshape.392 = bf16[32,24,4,768]{3,2,1,0:T(4,128)(2,1)} reshape(bf16[768,3072]{1,0:T(8,128)(2,1)} %slice.124) | data formatting | bytes 9437184 | tf_op jit(solution)/shard_map/reshape | solution.py:67
  153.7 5.5 copy.108
  159.2 4.0 fusion.20
  163.2 1.5 copy-done.5
  164.7 2.4 copy.101
  167.1 4.2 reshape.390
  176.3 2.2 fusion.132
  179.1 8.3 %fusion.6 = f32[512,6144]{1,0:T(8,128)S(1)} fusion(bf16[512,768]{1,0:T(8,128)(2,1)S(1)} %fusion.49, bf16[768,12288]{1,0:T(8,128)(2,1)} %all-gather.4.cloned.1.call-done), kind=kOutput, calls=%fused_computation.9 | convolution fusion | flops 4831838208 | bytes 22806528 | tf_op jit(solution)/shard_map/dot_general | solution.py:16
  187.5 28.4 %fusion.133 = (f32[512]{0:T(512)}, f32[512,768]{1,0:T(8,128)S(1)}) fusion(bf16[3072,768]{1,0:T(8,128)(2,1)S(1)} %bitcast.158, f32[512,6144]{1,0:T(8,128)S(1)} %fusion.6, f32[768]{0:T(1024)S(1)} %get-tuple-element.20, f32[768]{0:T(1024)S(1)} %get-tuple-element.21, f32[512]{0:T(512)S(1)} %add_rsqrt_fusion.3, f32[512,768]{1,0:T(8,128)S(1)} %get-tuple-element.37, ...), kind=kOutput, calls=%fused_computation.229 | convolution fusion | flops 2522086912 | bytes 20459520 | tf_op jit(solution)/shard_map/dot_general | solution.py:16
  224.7 5.3 fusion.4
  230.0 5.1 fusion.32
  235.4 6.7 %multiply_reduce_fusion.4 = (f32[768]{0:T(1024)}, f32[128]{0:T(128)S(1)}, f32[128]{0:T(128)S(1)}, f32[768]{0:T(1024)}, f32[128,768]{1,0:T(8,128)S(1)}) fusion(f32[4,32,768]{2,1,0:T(8,128)S(1)} %get-tuple-element.43, f32[128]{0:T(128)S(1)} %div.77, f32[128]{0:T(128)S(1)} %rsqrt.42, f32[768]{0:T(1024)S(1)} %get-tuple-element.21, f32[128,768]{1,0:T(8,128)S(1)} %fusion.67, ...), kind=kOutput, calls=%fused_computation.116 | convolution fusion | flops 1212086528 | bytes 12200960 | tf_op jit(solution)/shard_map/nf,df->nd/dot_general | solution.py:161
  243.1 1.9 convolution_convert_fusion.7
  248.4 3.9 fusion.43
  252.3 2.0 multiply_reduce_fusion.2
  255.8 5.3 convolution_convert_fusion
  264.8 1.5 copy.118
  267.7 2.3 copy.119
  270.0 3.1 copy.132
  275.6 5.2 fusion.19
  280.8 4.3 copy.120
  285.1 15.7 %pad_maximum_fusion = bf16[768,12288]{1,0:T(8,128)(2,1)} fusion(bf16[768,3072]{1,0:T(8,128)(2,1)} %bitcast.149, bf16[768,6144]{1,0:T(8,128)(2,1)} %convolution_convert_fusion, bf16[768,768]{1,0:T(8,128)(2,1)} %copy.121, bf16[768,2304]{1,0:T(8,128)(2,1)S(1)} %copy.120), kind=kLoop, calls=%fused_computation.2 | loop fusion | flops 75497472 | bytes 37748736 | tf_op jit(solution)/shard_map/concatenate | solution.py:88
  300.9 205.2 %reduce-scatter.2.cloned.1.call-done = bf16[24,12288]{1,0:T(8,128)(2,1)} async-done(((bf16[768,12288]{1,0:T(8,128)(2,1)}), bf16[24,12288]{1,0:T(8,128)(2,1)}) %reduce-scatter.2.cloned.1.call-update) | async-done | bytes 589840 | tf_op jit(solution)/shard_map/reduce_scatter | solution.py:89
  509.4 40.4 %psum.7 = f32[4,768]{1,0:T(4,128)} all-reduce(f32[4,768]{1,0:T(4,128)} %pad_maximum_fusion.7), channel_id=1, replica_groups=mesh['fsdp'=8,'dp'=4] {'fsdp','dp'}, use_global_device_ids=true, to_apply=%region_22.23 | all-reduce | flops 3072 | bytes 24576 | tf_op jit(solution)/shard_map/psum | solution.py:202
  552.2 1.5 fusion.76
  555.0 5.2 bitcast_add_fusion
  560.2 2.3 slice.133
  562.5 1.9 reshape.413
  567.3 1.6 slice.132
  (170 shorter events, 47.7 us)
Async XLA Ops:
  7.2 132.0 %all-gather.4.cloned.1.call-start = ((), (), s32[]{:S(2)}) async-start(), calls=%async_computation.1 | async-start | bytes 19464192 | tf_op jit(solution)/shard_map/all_gather | solution.py:64
  12.2 493.8 %reduce-scatter.2.cloned.1.call-start = ((), (), s32[]{:S(2)}) async-start(), calls=%async_computation.2 | async-start | bytes 19464192 | tf_op jit(solution)/shard_map/reduce_scatter | solution.py:89
  38.4 180.8 %copy-start.28 = (pred[4,32]{1,0:T(4,128)(4,1)}, pred[4,32]{1,0:T(4,128)(4,1)S(1)}, u32[]{:S(2)}) copy-start(pred[4,32]{1,0:T(4,128)(4,1)S(1)} %get-tuple-element.33) | copy-start | bytes 388
  153.7 5.5 copy-start.36
  178.8 8.7 %slice-start = ((s8[4718592]{0:T(1024)(128)(4,1)}), s8[4194304]{0:T(1024)(128)(4,1)S(1)}, s32[]{:S(2)}) async-start(s8[4718592]{0:T(1024)(128)(4,1)} %bitcast.156), calls=%async_computation.4 | async-start | bytes 8388608
  179.1 8.3 %copy-start.10 = (bf16[512,768]{1,0:T(8,128)(2,1)}, bf16[512,768]{1,0:T(8,128)(2,1)S(1)}, u32[]{:S(2)}) copy-start(bf16[512,768]{1,0:T(8,128)(2,1)S(1)} %fusion.49) | copy-start | bytes 2359300
  179.1 8.4 %slice-start.1 = ((s8[4718592]{0:T(1024)(128)(4,1)}), s8[524288]{0:T(1024)(128)(4,1)S(1)}, s32[]{:S(2)}) async-start(s8[4718592]{0:T(1024)(128)(4,1)} %bitcast.156), calls=%async_computation.5 | async-start | bytes 1048576
  187.5 29.6 %copy-start.26 = (s32[4,32]{1,0:T(4,128)S(1)}, s32[4,32]{1,0:T(4,128)}, u32[]{:S(2)}) copy-start(s32[4,32]{1,0:T(4,128)} %param.22) | copy-start | bytes 1540
  187.5 31.7 %copy-start.12 = (bf16[4,32,768]{2,1,0:T(8,128)(2,1)S(1)}, bf16[4,32,768]{2,1,0:T(8,128)(2,1)}, u32[]{:S(2)}) copy-start(bf16[4,32,768]{2,1,0:T(8,128)(2,1)} %param.21) | copy-start | bytes 589828
  222.9 12.4 %copy-start.34 = (f32[128]{0:T(128)}, f32[128]{0:T(128)S(1)}, u32[]{:S(2)}) copy-start(f32[128]{0:T(128)S(1)} %div.77) | copy-start | bytes 1540
  223.2 12.2 %copy-start.35 = (f32[128]{0:T(128)}, f32[128]{0:T(128)S(1)}, u32[]{:S(2)}) copy-start(f32[128]{0:T(128)S(1)} %rsqrt.42) | copy-start | bytes 1540
  224.7 5.3 copy-start.20
  230.0 5.2 copy-start.29
  230.0 5.2 copy-start.30
  230.0 5.2 copy-start.31
  230.0 5.1 copy-start.32
  230.0 5.1 copy-start.33
  235.2 7.0 %copy-start.22 = (bf16[128,3072]{1,0:T(8,128)(2,1)}, bf16[128,3072]{1,0:T(8,128)(2,1)S(1)}, u32[]{:S(2)}) copy-start(bf16[128,3072]{1,0:T(8,128)(2,1)S(1)} %get-tuple-element.22) | copy-start | bytes 2359300
  235.2 7.0 %copy-start.24 = (bf16[128,3072]{1,0:T(8,128)(2,1)}, bf16[128,3072]{1,0:T(8,128)(2,1)S(1)}, u32[]{:S(2)}) copy-start(bf16[128,3072]{1,0:T(8,128)(2,1)S(1)} %get-tuple-element.23) | copy-start | bytes 2359300
  242.2 3.2 slice-start.2
  243.1 30.5 %copy-start.3 = (f32[128,768]{1,0:T(8,128)}, f32[128,768]{1,0:T(8,128)S(1)}, u32[]{:S(2)}) copy-start(f32[128,768]{1,0:T(8,128)S(1)} %subtract_multiply_fusion) | copy-start | bytes 1179652
  255.8 5.3 copy-start.19
  261.8 13.7 %copy-start.14 = (bf16[96,8,4,128]{3,1,2,0:T(8,128)(2,1)}, bf16[96,8,4,128]{3,1,2,0:T(8,128)(2,1)S(1)}, u32[]{:S(2)}) copy-start(bf16[96,8,4,128]{3,1,2,0:T(8,128)(2,1)S(1)} %copy.163) | copy-start | bytes 2359300
  262.6 13.0 %copy-start.16 = (bf16[96,8,4,128]{3,1,2,0:T(8,128)(2,1)}, bf16[96,8,4,128]{3,1,2,0:T(8,128)(2,1)S(1)}, u32[]{:S(2)}) copy-start(bf16[96,8,4,128]{3,1,2,0:T(8,128)(2,1)S(1)} %copy.164) | copy-start | bytes 2359300
  300.8 250.6 %copy-start.1 = (f32[512,768]{1,0:T(8,128)S(1)}, f32[512,768]{1,0:T(8,128)}, u32[]{:S(2)}) copy-start(f32[512,768]{1,0:T(8,128)} %copy-done) | copy-start | bytes 4718596
  300.8 251.4 %copy-start.4 = (f32[128,768]{1,0:T(8,128)S(1)}, f32[128,768]{1,0:T(8,128)}, u32[]{:S(2)}) copy-start(f32[128,768]{1,0:T(8,128)} %copy-done.3) | copy-start | bytes 1179652
  300.8 253.0 %copy-start.27 = (f32[768]{0:T(1024)S(1)}, f32[768]{0:T(1024)}, u32[]{:S(2)}) copy-start(f32[768]{0:T(1024)} %get-tuple-element.19) | copy-start | bytes 9220
  300.8 254.2 %copy-start.15 = (bf16[96,8,4,128]{3,1,2,0:T(8,128)(2,1)S(1)}, bf16[96,8,4,128]{3,1,2,0:T(8,128)(2,1)}, u32[]{:S(2)}) copy-start(bf16[96,8,4,128]{3,1,2,0:T(8,128)(2,1)} %copy-done.14) | copy-start | bytes 2359300
  300.8 254.2 %copy-start.17 = (bf16[96,8,4,128]{3,1,2,0:T(8,128)(2,1)S(1)}, bf16[96,8,4,128]{3,1,2,0:T(8,128)(2,1)}, u32[]{:S(2)}) copy-start(bf16[96,8,4,128]{3,1,2,0:T(8,128)(2,1)} %copy-done.16) | copy-start | bytes 2359300
  300.8 259.3 %all-gather.6.cloned.1.call-start = ((), (), s32[]{:S(2)}) async-start(), calls=%async_computation.3 | async-start | bytes 2949120 | tf_op jit(solution)/shard_map/all_gather | solution.py:90
  549.9 5.1 copy-start.18
  560.2 5.4 copy-start.2
  (12 other events, 21.4 us)
Sparse Core Ops, SparseCore 0:
  12.4 126.7 all-gather.3
  300.9 205.0 reduce-scatter.1
  507.6 23.6 all-gather.5
where the time goes:
time: 586 us; the launch traced here: 576 us
  waiting for transfers between devices  304 us (52%)
  matrix products  94.3 us (16%)
  local copies, waits for them, and re-layouts  68.5 us (12%)
  blocking collectives  63 us (11%)
  other arithmetic  30.7 us (5%)
  between operations  15 us (3%)
    reduce_scatter x1, waiting for transfers between devices, scatter_grads(): mine = lax.psum_scatter(joined, AXES, scatter_dimension=0, tiled=True)  205 us
    all_gather x1, waiting for transfers between devices, gather_weights(): lax.all_gather(jnp.concatenate([joined, down], axis=1), AXES, axis=0, til...  99 us
    dot_general x5, matrix products, mm(): return jnp.dot(a, b, preferred_element_type=F32)  48.2 us
    psum x1, blocking collectives, on_device(): lax.psum(jnp.stack([g_gain_attn, g_shift_attn, g_gain_ffn, g_shift_ffn]),...  40.4 us
    all_gather x1, blocking collectives, on_device(): norms = lax.all_gather(norms, 'fsdp', axis=1, tiled=True).astype(F32)  22.6 us
    concatenate x1, other arithmetic, scatter_grads(): joined = jnp.concatenate([g_qkv, g_out, g_up, down], axis=1).astype(LOW)  15.7 us
  transfers between devices with their start and end apart: 3, of which 2 were waited for; matrix products, arithmetic and copies ran while one was open for 3% of the time, Pallas kernels for 0%

commit v1 on v0

--- a/solution.py
+++ b/solution.py
@@ -10,6 +10,11 @@
 F32 = jnp.float32
 LOW = jnp.bfloat16
 AXES = ("fsdp", "dp")
+
+
+def gather_by_exchange(array, axis, dim):
+    copies = jnp.concatenate([array] * lax.axis_size(axis), axis=dim)
+    return lax.all_to_all(copies, axis, dim, dim, tiled=True)
 
 
 def mm(a, b):
@@ -112,7 +117,7 @@
     tokens = seqs * length
     most = positions.shape[1]
     norms = jnp.stack([gain_attn, shift_attn, gain_ffn, shift_ffn])
-    norms = lax.all_gather(norms, "fsdp", axis=1, tiled=True).astype(F32)
+    norms = gather_by_exchange(norms, "fsdp", 1).astype(F32)
     w_qkv, w_out, w_up, w_down = gather_weights(w_qkv, w_out, w_up, w_down)
     live = jnp.arange(most, dtype=jnp.int32)[None, :] < counts[:, None]
     onehot = (positions[:, :, None] == jnp.arange(length, dtype=jnp.int32)).astype(F32)

time: 586 us -> 587 us (level)
  blocking collectives: 63 us -> 40.3 us
  waiting for transfers between devices: 304 us -> 319 us
  starting transfers between devices: 0.12 us -> 7.43 us
    all_gather x1 -> x0, blocking collectives: 22.6 us -> none  [on_device(): norms = lax.all_gather(norms, 'fsdp', axis=1, tiled=True).astype(F32)]
    all_gather x1, waiting for transfers between devices: 99 us -> 111 us  [gather_weights(): lax.all_gather(jnp.concatenate([joined, down], axis=1), AXES, axis=0, til...]
    all_to_all x0 -> x1, starting transfers between devices: none -> 7.31 us  [gather_by_exchange(): return lax.all_to_all(copies, axis, dim, dim, tiled=True)]
  transfers between devices with their start and end apart: 3 -> 4, of which waited for: 2 -> 3; matrix products, arithmetic and copies ran while one was open for 3% -> 4% of each run, Pallas kernels for 0% -> 0%
where the time goes in v1:
time: 587 us; the launch traced here: 576 us
  waiting for transfers between devices  319 us (54%)
  matrix products  94.3 us (16%)
  local copies, waits for them, and re-layouts  70.2 us (12%)
  blocking collectives  40.3 us (7%)
  other arithmetic  30.7 us (5%)
  between operations  15 us (3%)
  starting transfers between devices  7.43 us (1%)
    reduce_scatter x1, waiting for transfers between devices, scatter_grads(): mine = lax.psum_scatter(joined, AXES, scatter_dimension=0, tiled=True)  205 us
    all_gather x1, waiting for transfers between devices, gather_weights(): lax.all_gather(jnp.concatenate([joined, down], axis=1), AXES, axis=0, til...  111 us
    dot_general x5, matrix products, mm(): return jnp.dot(a, b, preferred_element_type=F32)  48.1 us
    psum x1, blocking collectives, on_device(): lax.psum(jnp.stack([g_gain_attn, g_shift_attn, g_gain_ffn, g_shift_ffn]),...  40.3 us
    concatenate x1, other arithmetic, scatter_grads(): joined = jnp.concatenate([g_qkv, g_out, g_up, down], axis=1).astype(LOW)  15.7 us
  transfers between devices with their start and end apart: 4, of which 3 were waited for; matrix products, arithmetic and copies ran while one was open for 4% of the time, Pallas kernels for 0%

profile of v1, /device:TPU:0, one launch (start us, length us, event | category | flops | bytes accessed | tf_op | source)
XLA Modules:
  0.0 576.4 jit_solution(15349918225113142681)
XLA Ops:
  13.8 7.3 %all-to-all-start = ((bf16[4,8,96]{2,0,1:T(4,128)(2,1)}), bf16[4,8,96]{2,0,1:T(4,128)(2,1)S(1)}, u32[]{:S(2)}, u32[]{:S(2)}) async-start(bf16[4,8,96]{2,0,1:T(4,128)(2,1)} %copy.83), calls=%async_computation | async-start | bytes 16384 | tf_op jit(solution)/shard_map/all_to_all | solution.py:17
  24.9 2.7 all-to-all-done
  28.4 110.6 %all-gather.3.cloned.1.call-done = bf16[768,12288]{1,0:T(8,128)(2,1)} async-done(((bf16[24,12288]{1,0:T(8,128)(2,1)}), bf16[768,12288]{1,0:T(8,128)(2,1)}) %all-gather.3.cloned.1.call-update) | async-done | bytes 18874384 | tf_op jit(solution)/shard_map/all_gather | solution.py:69
  139.1 4.8 slice.128
  143.9 9.7 %reshape.403 = bf16[32,24,4,768]{3,2,1,0:T(4,128)(2,1)} reshape(bf16[768,3072]{1,0:T(8,128)(2,1)} %slice.128) | data formatting | bytes 9437184 | tf_op jit(solution)/shard_map/reshape | solution.py:72
  153.6 5.5 copy.84
  159.1 4.0 fusion.20
  164.6 2.4 copy.77
  167.0 4.2 reshape.401
  176.2 2.2 fusion.132
  179.1 8.3 %fusion.6 = f32[512,6144]{1,0:T(8,128)S(1)} fusion(bf16[512,768]{1,0:T(8,128)(2,1)S(1)} %fusion.49, bf16[768,12288]{1,0:T(8,128)(2,1)} %all-gather.3.cloned.1.call-done), kind=kOutput, calls=%fused_computation.9 | convolution fusion | flops 4831838208 | bytes 22806528 | tf_op jit(solution)/shard_map/dot_general | solution.py:21
  187.5 28.4 %fusion.133 = (f32[512]{0:T(512)}, f32[512,768]{1,0:T(8,128)S(1)}) fusion(bf16[3072,768]{1,0:T(8,128)(2,1)S(1)} %bitcast.151, f32[512,6144]{1,0:T(8,128)S(1)} %fusion.6, f32[768]{0:T(1024)S(1)} %add.117, f32[768]{0:T(1024)S(1)} %mul.310, f32[512]{0:T(512)S(1)} %add_rsqrt_fusion.3, f32[512,768]{1,0:T(8,128)S(1)} %get-tuple-element.37, ...), kind=kOutput, calls=%fused_computation.228 | convolution fusion | flops 2522086912 | bytes 20459520 | tf_op jit(solution)/shard_map/dot_general | solution.py:21
  224.6 5.3 fusion.4
  230.0 5.1 fusion.32
  235.3 6.7 %multiply_reduce_fusion.4 = (f32[768]{0:T(1024)}, f32[128]{0:T(128)S(1)}, f32[128]{0:T(128)S(1)}, f32[768]{0:T(1024)}, f32[128,768]{1,0:T(8,128)S(1)}) fusion(f32[4,32,768]{2,1,0:T(8,128)S(1)} %get-tuple-element.43, f32[128]{0:T(128)S(1)} %div.77, f32[128]{0:T(128)S(1)} %rsqrt.42, f32[768]{0:T(1024)S(1)} %mul.310, f32[128,768]{1,0:T(8,128)S(1)} %fusion.67, ...), kind=kOutput, calls=%fused_computation.116 | convolution fusion | flops 1212086528 | bytes 12200960 | tf_op jit(solution)/shard_map/nf,df->nd/dot_general | solution.py:166
  243.0 1.9 convolution_convert_fusion.7
  248.3 3.9 fusion.43
  252.2 2.0 multiply_reduce_fusion.2
  255.7 5.3 convolution_convert_fusion
  264.7 1.5 copy.94
  267.6 2.3 copy.95
  270.0 3.1 copy.108
  275.5 5.2 fusion.19
  280.7 4.3 copy.96
  285.0 15.7 %pad_maximum_fusion = bf16[768,12288]{1,0:T(8,128)(2,1)} fusion(bf16[768,3072]{1,0:T(8,128)(2,1)} %bitcast.142, bf16[768,6144]{1,0:T(8,128)(2,1)} %convolution_convert_fusion, bf16[768,768]{1,0:T(8,128)(2,1)} %copy.97, bf16[768,2304]{1,0:T(8,128)(2,1)S(1)} %copy.96), kind=kLoop, calls=%fused_computation.2 | loop fusion | flops 75497472 | bytes 37748736 | tf_op jit(solution)/shard_map/concatenate | solution.py:93
  300.8 205.2 %reduce-scatter.2.cloned.1.call-done = bf16[24,12288]{1,0:T(8,128)(2,1)} async-done(((bf16[768,12288]{1,0:T(8,128)(2,1)}), bf16[24,12288]{1,0:T(8,128)(2,1)}) %reduce-scatter.2.cloned.1.call-update) | async-done | bytes 589840 | tf_op jit(solution)/shard_map/reduce_scatter | solution.py:94
  510.0 40.3 %psum.7 = f32[4,768]{1,0:T(4,128)} all-reduce(f32[4,768]{1,0:T(4,128)} %pad_maximum_fusion.7), channel_id=1, replica_groups=mesh['fsdp'=8,'dp'=4] {'fsdp','dp'}, use_global_device_ids=true, to_apply=%region_22.23 | all-reduce | flops 3072 | bytes 24576 | tf_op jit(solution)/shard_map/psum | solution.py:207
  552.7 1.6 fusion.76
  555.5 5.2 bitcast_add_fusion
  560.7 2.3 slice.137
  563.0 1.9 reshape.424
  567.8 1.6 slice.136
  (179 shorter events, 50.8 us)
Async XLA Ops:
  7.2 131.9 %all-gather.3.cloned.1.call-start = ((), (), s32[]{:S(2)}) async-start(), calls=%async_computation.2 | async-start | bytes 19464192 | tf_op jit(solution)/shard_map/all_gather | solution.py:69
  13.8 13.8 %all-to-all-start = ((bf16[4,8,96]{2,0,1:T(4,128)(2,1)}), bf16[4,8,96]{2,0,1:T(4,128)(2,1)S(1)}, u32[]{:S(2)}, u32[]{:S(2)}) async-start(bf16[4,8,96]{2,0,1:T(4,128)(2,1)} %copy.83), calls=%async_computation | async-start | bytes 16384 | tf_op jit(solution)/shard_map/all_to_all | solution.py:17
  21.1 484.9 %reduce-scatter.2.cloned.1.call-start = ((), (), s32[]{:S(2)}) async-start(), calls=%async_computation.3 | async-start | bytes 19464192 | tf_op jit(solution)/shard_map/reduce_scatter | solution.py:94
  22.6 196.6 %copy-start.29 = (pred[4,32]{1,0:T(4,128)(4,1)}, pred[4,32]{1,0:T(4,128)(4,1)S(1)}, u32[]{:S(2)}) copy-start(pred[4,32]{1,0:T(4,128)(4,1)S(1)} %get-tuple-element.33) | copy-start | bytes 388
  153.6 5.5 copy-start.37
  178.7 8.7 %slice-start = ((s8[4718592]{0:T(1024)(128)(4,1)}), s8[4194304]{0:T(1024)(128)(4,1)S(1)}, s32[]{:S(2)}) async-start(s8[4718592]{0:T(1024)(128)(4,1)} %bitcast.149), calls=%async_computation.5 | async-start | bytes 8388608
  179.0 8.3 %copy-start.10 = (bf16[512,768]{1,0:T(8,128)(2,1)}, bf16[512,768]{1,0:T(8,128)(2,1)S(1)}, u32[]{:S(2)}) copy-start(bf16[512,768]{1,0:T(8,128)(2,1)S(1)} %fusion.49) | copy-start | bytes 2359300
  179.1 8.4 %slice-start.1 = ((s8[4718592]{0:T(1024)(128)(4,1)}), s8[524288]{0:T(1024)(128)(4,1)S(1)}, s32[]{:S(2)}) async-start(s8[4718592]{0:T(1024)(128)(4,1)} %bitcast.149), calls=%async_computation.6 | async-start | bytes 1048576
  187.4 29.6 %copy-start.26 = (s32[4,32]{1,0:T(4,128)S(1)}, s32[4,32]{1,0:T(4,128)}, u32[]{:S(2)}) copy-start(s32[4,32]{1,0:T(4,128)} %param.22) | copy-start | bytes 1540
  187.4 31.7 %copy-start.12 = (bf16[4,32,768]{2,1,0:T(8,128)(2,1)S(1)}, bf16[4,32,768]{2,1,0:T(8,128)(2,1)}, u32[]{:S(2)}) copy-start(bf16[4,32,768]{2,1,0:T(8,128)(2,1)} %param.21) | copy-start | bytes 589828
  222.9 12.4 %copy-start.35 = (f32[128]{0:T(128)}, f32[128]{0:T(128)S(1)}, u32[]{:S(2)}) copy-start(f32[128]{0:T(128)S(1)} %div.77) | copy-start | bytes 1540
  223.2 12.2 %copy-start.36 = (f32[128]{0:T(128)}, f32[128]{0:T(128)S(1)}, u32[]{:S(2)}) copy-start(f32[128]{0:T(128)S(1)} %rsqrt.42) | copy-start | bytes 1540
  224.6 5.3 copy-start.20
  229.9 5.2 copy-start.30
  229.9 5.2 copy-start.31
  229.9 5.2 copy-start.32
  229.9 5.1 copy-start.33
  229.9 5.1 copy-start.34
  235.1 7.0 %copy-start.22 = (bf16[128,3072]{1,0:T(8,128)(2,1)}, bf16[128,3072]{1,0:T(8,128)(2,1)S(1)}, u32[]{:S(2)}) copy-start(bf16[128,3072]{1,0:T(8,128)(2,1)S(1)} %get-tuple-element.22) | copy-start | bytes 2359300
  235.1 7.0 %copy-start.24 = (bf16[128,3072]{1,0:T(8,128)(2,1)}, bf16[128,3072]{1,0:T(8,128)(2,1)S(1)}, u32[]{:S(2)}) copy-start(bf16[128,3072]{1,0:T(8,128)(2,1)S(1)} %get-tuple-element.23) | copy-start | bytes 2359300
  243.0 30.5 %copy-start.3 = (f32[128,768]{1,0:T(8,128)}, f32[128,768]{1,0:T(8,128)S(1)}, u32[]{:S(2)}) copy-start(f32[128,768]{1,0:T(8,128)S(1)} %subtract_multiply_fusion) | copy-start | bytes 1179652
  255.7 5.3 copy-start.19
  261.8 13.7 %copy-start.14 = (bf16[96,8,4,128]{3,1,2,0:T(8,128)(2,1)}, bf16[96,8,4,128]{3,1,2,0:T(8,128)(2,1)S(1)}, u32[]{:S(2)}) copy-start(bf16[96,8,4,128]{3,1,2,0:T(8,128)(2,1)S(1)} %copy.138) | copy-start | bytes 2359300
  262.5 13.0 %copy-start.16 = (bf16[96,8,4,128]{3,1,2,0:T(8,128)(2,1)}, bf16[96,8,4,128]{3,1,2,0:T(8,128)(2,1)S(1)}, u32[]{:S(2)}) copy-start(bf16[96,8,4,128]{3,1,2,0:T(8,128)(2,1)S(1)} %copy.139) | copy-start | bytes 2359300
  300.7 207.3 %copy-start.27 = (f32[768]{0:T(1024)S(1)}, f32[768]{0:T(1024)}, u32[]{:S(2)}) copy-start(f32[768]{0:T(1024)} %get-tuple-element.12) | copy-start | bytes 9220
  300.7 251.2 %copy-start.1 = (f32[512,768]{1,0:T(8,128)S(1)}, f32[512,768]{1,0:T(8,128)}, u32[]{:S(2)}) copy-start(f32[512,768]{1,0:T(8,128)} %copy-done) | copy-start | bytes 4718596
  300.7 252.0 %copy-start.4 = (f32[128,768]{1,0:T(8,128)S(1)}, f32[128,768]{1,0:T(8,128)}, u32[]{:S(2)}) copy-start(f32[128,768]{1,0:T(8,128)} %copy-done.3) | copy-start | bytes 1179652
  300.7 254.8 %copy-start.15 = (bf16[96,8,4,128]{3,1,2,0:T(8,128)(2,1)S(1)}, bf16[96,8,4,128]{3,1,2,0:T(8,128)(2,1)}, u32[]{:S(2)}) copy-start(bf16[96,8,4,128]{3,1,2,0:T(8,128)(2,1)} %copy-done.14) | copy-start | bytes 2359300
  300.7 254.8 %copy-start.17 = (bf16[96,8,4,128]{3,1,2,0:T(8,128)(2,1)S(1)}, bf16[96,8,4,128]{3,1,2,0:T(8,128)(2,1)}, u32[]{:S(2)}) copy-start(bf16[96,8,4,128]{3,1,2,0:T(8,128)(2,1)} %copy-done.16) | copy-start | bytes 2359300
  300.8 259.9 %all-gather.5.cloned.1.call-start = ((), (), s32[]{:S(2)}) async-start(), calls=%async_computation.4 | async-start | bytes 2949120 | tf_op jit(solution)/shard_map/all_gather | solution.py:95
  508.0 46.2 %copy-start.28 = (f32[768]{0:T(1024)S(1)}, f32[768]{0:T(1024)}, u32[]{:S(2)}) copy-start(f32[768]{0:T(1024)} %add.122) | copy-start | bytes 9220
  560.7 5.4 copy-start.2
  (14 other events, 29.7 us)
Sparse Core Ops, SparseCore 0:
  12.4 126.6 all-gather.2
  300.9 205.0 reduce-scatter.1
  507.5 23.8 all-gather.4
